TPU v7x, 128 devices: a whole 4x4x4 slice. The times are simulated.
128 devices in a mesh: dp: 16 (over z, y_lo, core), expert: 8 (over x, y_hi).
Axes of the slice: x: 4, y: 4 (y_hi: 2, y_lo: 2; y = y_hi * 2 + y_lo), z: 4, core: 2. Of those that a mesh axis runs over, the one named last changes fastest.
Arguments:
- tokens: bfloat16 [16384, 4096], P(('dp', 'expert')), may hold values from -6 to 6
- expert_ids: int32 [16384, 2], P(('dp', 'expert')), may hold values from 0 to 7, all different within a row; in each aligned block of 128 rows (0 to 127, 128 to 255, ...) at most 80 rows name the same one
- gate_probs: float32 [16384, 2], P(('dp', 'expert')), may hold values from 0.2 to 1
- gate_weight: bfloat16 [8, 4096, 1536], P('expert', 'dp'), may hold values from -0.09375 to 0.09375
- up_weight: bfloat16 [8, 4096, 1536], P('expert', 'dp'), may hold values from -0.09375 to 0.09375
- down_weight: bfloat16 [8, 1536, 4096], P('expert', None, 'dp'), may hold values from -0.15625 to 0.15625
Outputs:
- mixed: bfloat16 [16384, 4096], P(('dp', 'expert'))
Inputs may be any that keep to these rules, and one draw needn't show every extreme that they name: `expert_ids`: each token names 2 different experts. Among the 128 tokens of one device (aligned blocks of rows), no expert is named by more than 80 tokens, and in every draw some expert is named by exactly 80 tokens of some device.
All inputs are finite; a program needn't handle non-finite values.
Results may differ from a plain program's by a relative error of at most 0.0057.
Values may be sent and summed in bfloat16 or wider, within the bound.
A program may use at most 128 MiB of HBM per device.

v0:
```python
import jax
import jax.numpy as jnp
from jax import lax
from jax.sharding import PartitionSpec as P

CAP = 80


def on_device(tokens, expert_ids, gate_probs, gate_weight, up_weight, down_weight):
    tok_count, model_width = tokens.shape
    top_count = expert_ids.shape[1]
    groups = lax.axis_size("expert")
    total_rows = groups * CAP
    flat_ids = expert_ids.reshape(-1)
    onehot = (flat_ids[:, None] == jnp.arange(groups, dtype=jnp.int32)[None, :]).astype(jnp.int32)
    ranks = jnp.cumsum(onehot, axis=0) - 1
    rank_own = jnp.sum(ranks * onehot, axis=1)
    slot_index = flat_ids * CAP + rank_own
    counts = jnp.sum(onehot, axis=0)
    source_rows = jnp.arange(tok_count * top_count, dtype=jnp.int32) // top_count
    table = jnp.full((total_rows,), tok_count, jnp.int32).at[slot_index].set(source_rows)
    padded_tokens = jnp.concatenate([tokens, jnp.zeros((1, model_width), tokens.dtype)], axis=0)
    send_rows = padded_tokens[table]
    received, arrived = (
        lax.all_to_all(send_rows, "expert", split_axis=0, concat_axis=0, tiled=True),
        lax.all_to_all(counts[:, None], "expert", split_axis=0, concat_axis=0, tiled=True),
    )
    arrived = arrived[:, 0]
    gate_local = gate_weight[0]
    up_local = up_weight[0]
    down_local = down_weight[0]
    gate = jnp.dot(
        received,
        lax.all_gather(gate_local, "dp", axis=0, tiled=True),
        preferred_element_type=jnp.float32,
    )
    upper = jnp.dot(
        received,
        lax.all_gather(up_local, "dp", axis=0, tiled=True),
        preferred_element_type=jnp.float32,
    )
    hidden = (jax.nn.silu(gate) * upper).astype(jnp.bfloat16)
    outputs = jnp.dot(
        hidden,
        lax.all_gather(down_local, "dp", axis=1, tiled=True),
        preferred_element_type=jnp.float32,
    ).astype(jnp.bfloat16)
    returned = lax.all_to_all(outputs, "expert", split_axis=0, concat_axis=0, tiled=True)
    picked = returned[slot_index].astype(jnp.float32)
    weighted = picked * gate_probs.reshape(-1)[:, None]
    mixed = jnp.sum(weighted.reshape(tok_count, top_count, model_width), axis=1)
    return mixed.astype(jnp.bfloat16)


def solution(mesh):
    placed = (
        P(("dp", "expert"), None),
        P(("dp", "expert"), None),
        P(("dp", "expert"), None),
        P("expert", "dp", None),
        P("expert", "dp", None),
        P("expert", None, "dp"),
    )
    return jax.shard_map(
        on_device, mesh=mesh, in_specs=placed, out_specs=P(("dp", "expert"), None), check_vma=False
    )
```

profile of v0, /device:TPU:1, one launch (start us, length us, event | category | flops | bytes accessed | tf_op | source)
XLA Modules:
  0.0 431.1 jit_solution(3689289020772454636)
XLA Ops:
  6.5 0.7 all-gather.7.cloned.1.call-update
  7.3 0.7 all-gather.11.cloned.1.call-update
  8.1 0.7 all-gather.9.cloned.1.call-update
  8.7 0.8 copy.9
  9.5 0.1 eq.29
  9.7 0.1 eq.25
  9.8 0.6 reduce-window.6
  10.4 0.2 slice_reduce_fusion
  10.7 0.7 broadcast_multiply_fusion
  11.5 0.1 mul.37
  11.6 1.3 concatenate.3
  13.1 1.4 scatter_custom_fusion
  14.5 5.4 %gather_fusion = bf16[640,4096]{1,0:T(8,128)(2,1)} fusion(bf16[129,4096]{1,0:T(8,128)(2,1)S(1)} %concatenate.3, s32[1024]{0:T(1024)S(1)} %pad_clamp_fusion.1), kind=kCustom, calls=%fused_computation | custom fusion | bytes 10488320 | tf_op jit(solution)/shard_map/gather | solution.py:23
  19.9 81.7 %all_to_all.24 = bf16[8,80,4096]{2,1,0:T(8,128)(2,1)} all-to-all(bf16[8,80,4096]{2,1,0:T(8,128)(2,1)} %bitcast.29), channel_id=1, replica_groups=mesh['dp'=16,'expert'=8] {'expert'}, dimensions={0} | all-to-all | bytes 10485760 | tf_op jit(solution)/shard_map/all_to_all | solution.py:25
  101.6 39.0 %all-gather.7.cloned.1.call-done = bf16[1,4096,1536]{2,1,0:T(8,128)(2,1)} async-done(((bf16[1,256,1536]{2,1,0:T(8,128)(2,1)}), bf16[1,4096,1536]{2,1,0:T(8,128)(2,1)}) %all-gather.7.cloned.1.call-update) | async-done | bytes 12582928 | tf_op jit(solution)/shard_map/all_gather | solution.py:34
  140.6 14.1 %fusion.4 = f32[640,1536]{1,0:T(8,128)} fusion(bf16[640,4096]{1,0:T(8,128)(2,1)} %bitcast.30, bf16[1,4096,1536]{2,1,0:T(8,128)(2,1)} %all-gather.7.cloned.1.call-done), kind=kOutput, calls=%fused_computation.7 | convolution fusion | flops 8053063680 | bytes 21757952 | tf_op jit(solution)/shard_map/dot_general | solution.py:32
  154.7 67.9 %all-gather.11.cloned.1.call-done = bf16[1,1536,4096]{2,1,0:T(8,128)(2,1)} async-done(((bf16[1,1536,256]{2,1,0:T(8,128)(2,1)}), bf16[1,1536,4096]{2,1,0:T(8,128)(2,1)}) %all-gather.11.cloned.1.call-update) | async-done | bytes 12582928 | tf_op jit(solution)/shard_map/all_gather | solution.py:45
  222.6 73.6 %all-gather.9.cloned.1.call-done = bf16[1,4096,1536]{2,1,0:T(8,128)(2,1)} async-done(((bf16[1,256,1536]{2,1,0:T(8,128)(2,1)}), bf16[1,4096,1536]{2,1,0:T(8,128)(2,1)}) %all-gather.9.cloned.1.call-update) | async-done | bytes 12582928 | tf_op jit(solution)/shard_map/all_gather | solution.py:39
  296.2 27.9 %fusion.6 = bf16[640,4096]{1,0:T(8,128)(2,1)} fusion(bf16[1,1536,4096]{2,1,0:T(8,128)(2,1)} %all-gather.11.cloned.1.call-done, f32[640,1536]{1,0:T(8,128)} %fusion.4, bf16[640,4096]{1,0:T(8,128)(2,1)} %bitcast.31, bf16[1,4096,1536]{2,1,0:T(8,128)(2,1)} %all-gather.9.cloned.1.call-done), kind=kOutput, calls=%fused_computation.9 | convolution fusion | flops 16114647040 | bytes 39583744 | tf_op jit(solution)/shard_map/dot_general | solution.py:43
  324.1 6.6 %all-to-all-start.1 = ((bf16[8,80,4096]{2,1,0:T(8,128)(2,1)}), bf16[8,80,4096]{2,1,0:T(8,128)(2,1)}, u32[]{:S(2)}, u32[]{:S(2)}) async-start(bf16[8,80,4096]{2,1,0:T(8,128)(2,1)} %bitcast.32), calls=%async_computation.1 | async-start | bytes 10485760 | tf_op jit(solution)/shard_map/all_to_all | solution.py:48
  330.8 73.1 %all-to-all-done.1 = bf16[8,80,4096]{2,1,0:T(8,128)(2,1)} async-done(((bf16[8,80,4096]{2,1,0:T(8,128)(2,1)}), bf16[8,80,4096]{2,1,0:T(8,128)(2,1)}, u32[]{:S(2)}, u32[]{:S(2)}) %all-to-all-start.1) | async-done | bytes 5242912 | tf_op jit(solution)/shard_map/all_to_all | solution.py:48
  403.9 7.0 %gather_fusion.1 = bf16[256,4096]{1,0:T(8,128)(2,1)S(1)} fusion(bf16[640,4096]{1,0:T(8,128)(2,1)} %bitcast.10, s32[1024]{0:T(1024)S(1)} %pad_clamp_fusion), kind=kCustom, calls=%fused_computation.1 | custom fusion | bytes 4195328 | tf_op jit(solution)/shard_map/gather | solution.py:49
  410.9 4.0 reshape.63
  414.9 9.6 %multiply_reduce_fusion = bf16[128,4096]{1,0:T(8,128)(2,1)} fusion(f32[128,2,4096]{2,1,0:T(2,128)} %reshape.63, f32[128,2]{1,0:T(8,128)S(1)} %copy.11), kind=kLoop, calls=%fused_computation.10 | loop fusion | flops 1572864 | bytes 5243904 | tf_op jit(solution)/shard_map/reduce_sum | solution.py:51
  (20 shorter events, 0.5 us)
Async XLA Ops:
  6.5 134.1 %all-gather.7.cloned.1.call-start = ((), (), s32[]{:S(2)}) async-start(), calls=%async_computation.2 | async-start | bytes 13369344 | tf_op jit(solution)/shard_map/all_gather | solution.py:34
  7.3 215.4 %all-gather.11.cloned.1.call-start = ((), (), s32[]{:S(2)}) async-start(), calls=%async_computation.4 | async-start | bytes 13369344 | tf_op jit(solution)/shard_map/all_gather | solution.py:45
  8.0 288.2 %all-gather.9.cloned.1.call-start = ((), (), s32[]{:S(2)}) async-start(), calls=%async_computation.3 | async-start | bytes 13369344 | tf_op jit(solution)/shard_map/all_gather | solution.py:39
  13.1 6.9 %copy-start = (s32[256,1]{0,1:T(1,128)}, s32[256,1]{0,1:T(1,128)S(1)}, u32[]{:S(2)}) copy-start(s32[256,1]{0,1:T(1,128)S(1)} %compare_select_fusion.1) | copy-start | bytes 3076
  324.1 6.6 %copy-start.2 = (f32[128,2]{0,1:T(2,128)S(1)}, f32[128,2]{0,1:T(2,128)}, u32[]{:S(2)}) copy-start(f32[128,2]{0,1:T(2,128)} %param.8) | copy-start | bytes 3076
  324.1 6.7 %copy-start.1 = (s32[256,1]{0,1:T(1,128)S(1)}, s32[256,1]{0,1:T(1,128)}, u32[]{:S(2)}) copy-start(s32[256,1]{0,1:T(1,128)} %copy-done) | copy-start | bytes 3076
  324.1 79.8 %all-to-all-start.1 = ((bf16[8,80,4096]{2,1,0:T(8,128)(2,1)}), bf16[8,80,4096]{2,1,0:T(8,128)(2,1)}, u32[]{:S(2)}, u32[]{:S(2)}) async-start(bf16[8,80,4096]{2,1,0:T(8,128)(2,1)} %bitcast.32), calls=%async_computation.1 | async-start | bytes 10485760 | tf_op jit(solution)/shard_map/all_to_all | solution.py:48
Sparse Core Ops, SparseCore 0:
  9.1 131.5 all-gather.6
  142.2 80.3 all-gather.10
  224.3 71.8 all-gather.8
where the time goes:
time: 432 us; the launch traced here: 431 us
  waiting for transfers between devices  256 us (59%)
  blocking collectives  81.7 us (19%)
  matrix products  41.9 us (10%)
  local copies, waits for them, and re-layouts  20.8 us (5%)
  between operations  13.2 us (3%)
  other arithmetic  11.1 us (3%)
  starting transfers between devices  6.64 us (2%)
    all_to_all x1, blocking collectives, on_device(): lax.all_to_all(send_rows, 'expert', split_axis=0, concat_axis=0, tiled=True)  81.7 us
    all_gather x1, waiting for transfers between devices, on_device(): lax.all_gather(up_local, 'dp', axis=0, tiled=True)  73.6 us
    all_to_all x1, waiting for transfers between devices, on_device(): lax.all_to_all(outputs, 'expert', split_axis=0, concat_axis=0, tiled=True)  73.1 us
    all_gather x1, waiting for transfers between devices, on_device(): lax.all_gather(down_local, 'dp', axis=1, tiled=True)  67.9 us
    all_gather x1, waiting for transfers between devices, on_device(): lax.all_gather(gate_local, 'dp', axis=0, tiled=True)  39 us
    dot_general x1, matrix products, on_device(): jnp.dot(hidden, lax.all_gather(down_local, 'dp', axis=1, tiled=True), pre...  27.9 us
    dot_general x1, matrix products, on_device(): jnp.dot(received, lax.all_gather(gate_local, 'dp', axis=0, tiled=True), p...  14.1 us
    reduce_sum x1, other arithmetic, on_device(): mixed = jnp.sum(weighted.reshape(tok_count, top_count, model_width), axis=1)  9.64 us
  transfers between devices with their start and end apart: 4, of which 4 were waited for; matrix products, arithmetic and copies ran while one was open for 6% of the time, Pallas kernels for 0%

commit v1 on v0

--- a/solution.py
+++ b/solution.py
@@ -42,7 +42,9 @@
     hidden = (jax.nn.silu(gate) * upper).astype(jnp.bfloat16)
     outputs = jnp.dot(
         hidden,
-        lax.all_gather(down_local, "dp", axis=1, tiled=True),
+        jnp.concatenate(
+            lax.all_to_all(jnp.stack([down_local] * lax.axis_size("dp")), "dp", 0, 0), axis=1
+        ),
         preferred_element_type=jnp.float32,
     ).astype(jnp.bfloat16)
     returned = lax.all_to_all(outputs, "expert", split_axis=0, concat_axis=0, tiled=True)

time: 432 us -> 492 us (1.14)
  waiting for transfers between devices: 256 us -> 370 us
  blocking collectives: 81.7 us -> 0 us
  starting transfers between devices: 6.64 us -> 24.3 us
  local copies, waits for them, and re-layouts: 20.8 us -> 26.9 us
    all_to_all x0 -> x2, waiting for transfers between devices: none -> 223 us  [the longest x1 149 us: on_device(): lax.all_to_all(jnp.stack([down_local] * lax.axis_size('dp')), 'dp', 0, 0)]
    all_to_all x1 -> x0, blocking collectives: 81.7 us -> none  [on_device(): lax.all_to_all(send_rows, 'expert', split_axis=0, concat_axis=0, tiled=True)]
    all_gather x1 -> x0, waiting for transfers between devices: 67.9 us -> none  [on_device(): lax.all_gather(down_local, 'dp', axis=1, tiled=True)]
    all_gather x1, waiting for transfers between devices: 73.6 us -> 6.45 us  [on_device(): lax.all_gather(up_local, 'dp', axis=0, tiled=True)]
    all_gather x1, waiting for transfers between devices: 39 us -> 66.8 us  [on_device(): lax.all_gather(gate_local, 'dp', axis=0, tiled=True)]
    all_to_all x0 -> x2, starting transfers between devices: none -> 14.9 us  [the longest x1 7.61 us: on_device(): lax.all_to_all(send_rows, 'expert', split_axis=0, concat_axis=0, tiled=True)]
    another operation x1 -> x3, local copies, waits for them, and re-layouts: 0.01 us -> 5.94 us  [the longest x1 5.66 us: on_device(): jnp.stack([down_local] * lax.axis_size('dp'))]
  transfers between devices with their start and end apart: 4 -> 5, of which waited for: 4 -> 5; matrix products, arithmetic and copies ran while one was open for 6% -> 6% of each run, Pallas kernels for 0% -> 0%
where the time goes in v1:
time: 492 us; the launch traced here: 486 us
  waiting for transfers between devices  370 us (75%)
  matrix products  40.2 us (8%)
  local copies, waits for them, and re-layouts  26.9 us (5%)
  starting transfers between devices  24.3 us (5%)
  between operations  13.5 us (3%)
  other arithmetic  11.1 us (2%)
    all_to_all x1, waiting for transfers between devices, on_device(): lax.all_to_all(jnp.stack([down_local] * lax.axis_size('dp')), 'dp', 0, 0)  149 us
    all_to_all x1, waiting for transfers between devices, on_device(): lax.all_to_all(send_rows, 'expert', split_axis=0, concat_axis=0, tiled=True)  74 us
    all_to_all x1, waiting for transfers between devices, on_device(): lax.all_to_all(outputs, 'expert', split_axis=0, concat_axis=0, tiled=True)  72.7 us
    all_gather x1, waiting for transfers between devices, on_device(): lax.all_gather(gate_local, 'dp', axis=0, tiled=True)  66.8 us
    dot_general x1, matrix products, on_device(): jnp.dot(hidden, jnp.concatenate(lax.all_to_all(jnp.stack([down_local] * l...  26.1 us
    dot_general x1, matrix products, on_device(): jnp.dot(received, lax.all_gather(gate_local, 'dp', axis=0, tiled=True), p...  14.1 us
  transfers between devices with their start and end apart: 5, of which 5 were waited for; matrix products, arithmetic and copies ran while one was open for 6% of the time, Pallas kernels for 0%

profile of v1, /device:TPU:1, one launch (start us, length us, event | category | flops | bytes accessed | tf_op | source)
XLA Modules:
  0.0 486.2 jit_solution(11354025230426715989)
XLA Ops:
  6.5 0.7 all-gather.5.cloned.1.call-update
  7.3 0.7 all-gather.7.cloned.1.call-update
  8.0 0.8 copy.9
  9.1 0.6 reduce-window.6
  9.7 0.2 slice_reduce_fusion
  9.9 0.7 broadcast_multiply_fusion
  10.9 1.3 concatenate.3
  12.3 1.4 scatter_custom_fusion
  13.8 5.5 %gather_fusion = bf16[640,4096]{1,0:T(8,128)(2,1)} fusion(bf16[129,4096]{1,0:T(8,128)(2,1)S(1)} %concatenate.3, s32[1024]{0:T(1024)S(1)} %pad_clamp_fusion.1), kind=kCustom, calls=%fused_computation | custom fusion | bytes 10488320 | tf_op jit(solution)/shard_map/gather | solution.py:23
  19.3 7.6 %all-to-all-start = ((bf16[8,80,4096]{2,1,0:T(8,128)(2,1)}), bf16[8,80,4096]{2,1,0:T(8,128)(2,1)}, u32[]{:S(2)}, u32[]{:S(2)}) async-start(bf16[8,80,4096]{2,1,0:T(8,128)(2,1)} %bitcast.29), calls=%async_computation | async-start | bytes 10485760 | tf_op jit(solution)/shard_map/all_to_all | solution.py:25
  26.9 0.3 copy.11
  27.2 74.0 %all-to-all-done = bf16[8,80,4096]{2,1,0:T(8,128)(2,1)} async-done(((bf16[8,80,4096]{2,1,0:T(8,128)(2,1)}), bf16[8,80,4096]{2,1,0:T(8,128)(2,1)}, u32[]{:S(2)}, u32[]{:S(2)}) %all-to-all-start) | async-done | bytes 5242912 | tf_op jit(solution)/shard_map/all_to_all | solution.py:25
  101.1 5.7 %stack.3 = bf16[16,1536,256]{1,2,0:T(8,128)(2,1)} broadcast(bf16[1536,256]{0,1:T(8,128)(2,1)S(1)} %copy.11), dimensions={1,2} | broadcast | bytes 13369344 | tf_op jit(solution)/shard_map/stack | solution.py:46
  106.8 7.2 %all-to-all-start.1 = ((bf16[16,1536,256]{1,2,0:T(8,128)(2,1)}), bf16[16,1536,256]{1,2,0:T(8,128)(2,1)}, u32[]{:S(2)}, u32[]{:S(2)}) async-start(bf16[16,1536,256]{1,2,0:T(8,128)(2,1)} %stack.3), calls=%async_computation.1 | async-start | bytes 25165824 | tf_op jit(solution)/shard_map/all_to_all | solution.py:46
  114.0 66.8 %all-gather.5.cloned.1.call-done = bf16[1,4096,1536]{2,1,0:T(8,128)(2,1)} async-done(((bf16[1,256,1536]{2,1,0:T(8,128)(2,1)}), bf16[1,4096,1536]{2,1,0:T(8,128)(2,1)}) %all-gather.5.cloned.1.call-update) | async-done | bytes 12582928 | tf_op jit(solution)/shard_map/all_gather | solution.py:34
  180.8 14.1 %fusion.2 = f32[640,1536]{1,0:T(8,128)} fusion(bf16[640,4096]{1,0:T(8,128)(2,1)} %bitcast.5, bf16[1,4096,1536]{2,1,0:T(8,128)(2,1)} %all-gather.5.cloned.1.call-done), kind=kOutput, calls=%fused_computation.5 | convolution fusion | flops 8053063680 | bytes 21757952 | tf_op jit(solution)/shard_map/dot_general | solution.py:32
  195.0 148.9 %all-to-all-done.1 = bf16[16,1536,256]{1,2,0:T(8,128)(2,1)} async-done(((bf16[16,1536,256]{1,2,0:T(8,128)(2,1)}), bf16[16,1536,256]{1,2,0:T(8,128)(2,1)}, u32[]{:S(2)}, u32[]{:S(2)}) %all-to-all-start.1) | async-done | bytes 12582944 | tf_op jit(solution)/shard_map/all_to_all | solution.py:46
  343.9 6.5 %all-gather.7.cloned.1.call-done = bf16[1,4096,1536]{2,1,0:T(8,128)(2,1)} async-done(((bf16[1,256,1536]{2,1,0:T(8,128)(2,1)}), bf16[1,4096,1536]{2,1,0:T(8,128)(2,1)}) %all-gather.7.cloned.1.call-update) | async-done | bytes 12582928 | tf_op jit(solution)/shard_map/all_gather | solution.py:39
  350.4 26.1 %convolution_convert_fusion = bf16[640,4096]{1,0:T(8,128)(2,1)} fusion(bf16[1536,4096]{0,1:T(8,128)(2,1)} %bitcast.10, f32[640,1536]{1,0:T(8,128)} %fusion.2, bf16[640,4096]{1,0:T(8,128)(2,1)} %bitcast.5, bf16[1,4096,1536]{2,1,0:T(8,128)(2,1)} %all-gather.7.cloned.1.call-done), kind=kOutput, calls=%fused_computation.7 | convolution fusion | flops 16114647040 | bytes 39583744 | tf_op jit(solution)/shard_map/dot_general | solution.py:43
  376.4 9.4 %all-to-all-start.2 = ((bf16[8,80,4096]{2,1,0:T(8,128)(2,1)}), bf16[8,80,4096]{2,1,0:T(8,128)(2,1)}, u32[]{:S(2)}, u32[]{:S(2)}) async-start(bf16[8,80,4096]{2,1,0:T(8,128)(2,1)} %bitcast.30), calls=%async_computation.2 | async-start | bytes 10485760 | tf_op jit(solution)/shard_map/all_to_all | solution.py:50
  386.0 72.7 %all-to-all-done.2 = bf16[8,80,4096]{2,1,0:T(8,128)(2,1)} async-done(((bf16[8,80,4096]{2,1,0:T(8,128)(2,1)}), bf16[8,80,4096]{2,1,0:T(8,128)(2,1)}, u32[]{:S(2)}, u32[]{:S(2)}) %all-to-all-start.2) | async-done | bytes 5242912 | tf_op jit(solution)/shard_map/all_to_all | solution.py:50
  458.7 7.0 %gather_fusion.1 = bf16[256,4096]{1,0:T(8,128)(2,1)S(1)} fusion(bf16[640,4096]{1,0:T(8,128)(2,1)} %bitcast.12, s32[1024]{0:T(1024)S(1)} %pad_clamp_fusion), kind=kCustom, calls=%fused_computation.1 | custom fusion | bytes 4195328 | tf_op jit(solution)/shard_map/gather | solution.py:51
  465.8 4.0 reshape.72
  469.8 9.6 %multiply_reduce_fusion = bf16[128,4096]{1,0:T(8,128)(2,1)} fusion(f32[128,2,4096]{2,1,0:T(2,128)} %reshape.72, f32[128,2]{1,0:T(8,128)S(1)} %copy.12), kind=kLoop, calls=%fused_computation.8 | loop fusion | flops 1572864 | bytes 5243904 | tf_op jit(solution)/shard_map/reduce_sum | solution.py:53
  (24 shorter events, 0.9 us)
Async XLA Ops:
  6.5 174.3 %all-gather.5.cloned.1.call-start = ((), (), s32[]{:S(2)}) async-start(), calls=%async_computation.3 | async-start | bytes 13369344 | tf_op jit(solution)/shard_map/all_gather | solution.py:34
  7.3 343.1 %all-gather.7.cloned.1.call-start = ((), (), s32[]{:S(2)}) async-start(), calls=%async_computation.4 | async-start | bytes 13369344 | tf_op jit(solution)/shard_map/all_gather | solution.py:39
  12.3 6.9 %copy-start.1 = (s32[256,1]{0,1:T(1,128)}, s32[256,1]{0,1:T(1,128)S(1)}, u32[]{:S(2)}) copy-start(s32[256,1]{0,1:T(1,128)S(1)} %compare_select_fusion.1) | copy-start | bytes 3076
  19.3 7.6 %copy-start = (bf16[1,1536,256]{2,1,0:T(8,128)(2,1)S(1)}, bf16[1,1536,256]{2,1,0:T(8,128)(2,1)}, u32[]{:S(2)}) copy-start(bf16[1,1536,256]{2,1,0:T(8,128)(2,1)} %param.11) | copy-start | bytes 2359300
  19.3 81.8 %all-to-all-start = ((bf16[8,80,4096]{2,1,0:T(8,128)(2,1)}), bf16[8,80,4096]{2,1,0:T(8,128)(2,1)}, u32[]{:S(2)}, u32[]{:S(2)}) async-start(bf16[8,80,4096]{2,1,0:T(8,128)(2,1)} %bitcast.29), calls=%async_computation | async-start | bytes 10485760 | tf_op jit(solution)/shard_map/all_to_all | solution.py:25
  106.8 237.1 %all-to-all-start.1 = ((bf16[16,1536,256]{1,2,0:T(8,128)(2,1)}), bf16[16,1536,256]{1,2,0:T(8,128)(2,1)}, u32[]{:S(2)}, u32[]{:S(2)}) async-start(bf16[16,1536,256]{1,2,0:T(8,128)(2,1)} %stack.3), calls=%async_computation.1 | async-start | bytes 25165824 | tf_op jit(solution)/shard_map/all_to_all | solution.py:46
  376.4 9.4 %copy-start.3 = (f32[128,2]{0,1:T(2,128)S(1)}, f32[128,2]{0,1:T(2,128)}, u32[]{:S(2)}) copy-start(f32[128,2]{0,1:T(2,128)} %param.8) | copy-start | bytes 3076
  376.4 9.6 %copy-start.2 = (s32[256,1]{0,1:T(1,128)S(1)}, s32[256,1]{0,1:T(1,128)}, u32[]{:S(2)}) copy-start(s32[256,1]{0,1:T(1,128)} %copy-done.1) | copy-start | bytes 3076
  376.4 82.3 %all-to-all-start.2 = ((bf16[8,80,4096]{2,1,0:T(8,128)(2,1)}), bf16[8,80,4096]{2,1,0:T(8,128)(2,1)}, u32[]{:S(2)}, u32[]{:S(2)}) async-start(bf16[8,80,4096]{2,1,0:T(8,128)(2,1)} %bitcast.30), calls=%async_computation.2 | async-start | bytes 10485760 | tf_op jit(solution)/shard_map/all_to_all | solution.py:50
Sparse Core Ops, SparseCore 0:
  9.1 171.7 all-gather.4
  182.5 167.7 all-gather.6
